TPU v7x, 128 devices: a whole 4x4x4 slice. The times are simulated.
128 devices in a mesh: gx: 8 (over y, core), gy: 16 (over x, z).
Axes of the slice: x: 4, y: 4, z: 4, core: 2. Of those that a mesh axis runs over, the one named last changes fastest.
Arguments:
- hblocks: float32 [8, 16, 9, 128, 128], P('gx', 'gy'), may hold values from -1 to 1, as said below
- onsite: float32 [8, 16, 128], P('gx', 'gy'), may hold values from -1.5 to 1.5
- pattern: int32 [8, 16, 9], P('gx', 'gy'), may hold values 0 or 1
- slot_code: int32 [8, 16, 6], P('gx', 'gy'), may hold values from 0 to 9, as said below
- basis: bfloat16 [8, 16, 9, 1024, 128], P('gx', 'gy'), may hold values from -0.5 to 0.5
Outputs:
- density: bfloat16 [8, 16, 9, 128, 128], P('gx', 'gy')
- grid_density: float32 [8, 16, 1024], P('gx', 'gy')
Inputs may be any that keep to these rules, and one draw needn't show every extreme that they name: `hblocks`: standard deviations differ between block columns. `slot_code`: slot 0 of every column holds 4, the block itself; the next slots hold distinct codes other than 4, and the remaining slots hold 9 (unused). Every column uses 2 or more slots, and in every draw some column uses all 6.
All inputs are finite; a program needn't handle non-finite values. No bound on the sum of `pattern` on one device may be relied on, other than what follows from the above.
Results may differ from a plain program's by a relative error of at most 0.001.
Values may be sent and summed in bfloat16 or wider, within the bound.
A program may use at most 128 MiB of HBM per device.

v0:
```python
import functools

import jax
import jax.numpy as jnp
from jax import lax
from jax.experimental import pallas as pl
from jax.experimental.pallas import tpu as pltpu
from jax.sharding import PartitionSpec as P

POWER_STEPS = 6
B = 128
SLOTS = 6
ORDER = SLOTS * B
MESH = pl.DeviceIdType.MESH
F32 = jnp.float32
BF16 = jnp.bfloat16

BELOW_X, ABOVE_X, BELOW_Y, ABOVE_Y = 1, 7, 3, 5


def needed(place):
    spans = (slice(1, 3), slice(0, 3), slice(0, 2))
    return spans[place // 3], spans[place % 3]


def split(value):
    high = value.astype(BF16)
    return high, (value - high.astype(F32)).astype(BF16)


def exchange(hood, sends, recvs, base, gx, gy, n_gx, n_gy):
    up_x = (lax.rem(gx + 1, n_gx), gy)
    down_x = (lax.rem(gx + n_gx - 1, n_gx), gy)
    up_y = (gx, lax.rem(gy + 1, n_gy))
    down_y = (gx, lax.rem(gy + n_gy - 1, n_gy))

    def copy(index, source, target, rows, columns, device):
        return pltpu.make_async_remote_copy(
            src_ref=hood.at[source, rows, columns],
            dst_ref=hood.at[target, rows, columns],
            send_sem=sends.at[index],
            recv_sem=recvs.at[index],
            device_id=device,
            device_id_type=MESH,
        )

    copies = {}
    index = base
    for row in (1, 0, 2):
        for place, device in ((BELOW_Y, up_y), (ABOVE_Y, down_y)):
            columns = needed(place)[1]
            copies[place, row] = copy(index, 4, place, slice(row, row + 1), columns, device)
            index += 1
    for place, device in ((BELOW_X, up_x), (ABOVE_X, down_x)):
        rows, columns = needed(place)
        copies[place] = copy(index, 4, place, rows, columns, device)
        index += 1
    for row in (1, 0, 2):
        for source in (BELOW_Y, ABOVE_Y):
            for shift, device in ((-1, up_x), (1, down_x)):
                place = source + 3 * shift
                rows, columns = needed(place)
                if rows.start <= row < rows.stop:
                    copies[place, row] = copy(
                        index, source, place, slice(row, row + 1), columns, device
                    )
                    index += 1
    return copies


COPIES = 16


def begin(copies):
    for row in (1, 0, 2):
        for place in (BELOW_Y, ABOVE_Y):
            copies[place, row].start()
    for place in (BELOW_X, ABOVE_X):
        copies[place].start()


def forward(copies, row):
    for source in (BELOW_Y, ABOVE_Y):
        copies[source, row].wait_recv()
        for place in (source - 3, source + 3):
            if (place, row) in copies:
                copies[place, row].start()


def three(left, right):
    lhs = jnp.concatenate([left[0], left[0], left[1]], axis=1)
    rhs = jnp.concatenate([right[0], right[1], right[0]], axis=0)
    return jnp.dot(lhs, rhs, preferred_element_type=F32)


def thin(matrix, high, low):
    rhs = jnp.concatenate([high, low], axis=1)
    out = []
    for start in range(0, ORDER, 256):
        rows = slice(start, start + 256)
        both = jnp.dot(matrix[0][rows, :], rhs, preferred_element_type=F32)
        rest = jnp.dot(matrix[1][rows, :], high, preferred_element_type=F32)
        out.append(both[:, :B] + (both[:, B:] + rest))
    return jnp.concatenate(out, axis=0)


def kernel(
    n_gx, n_gy,
    h_any, onsite_ref, pattern_ref, code_ref, basis_any,
    density_ref, grid_ref,
    h_buf, basis, hood, m_f, m_hi, m_lo, q_hi, q_lo, n_f, x_hi, x_lo,
    column, halves, dhood, grid_acc, best, best_x, best_y,
    in_sem, sends, recvs, sends_x, recvs_x, sends_y, recvs_y,
):
    gx, gy = lax.axis_index("gx"), lax.axis_index("gy")

    load_h = pltpu.make_async_copy(h_any.at[0, 0], h_buf, in_sem.at[0])
    load_h.start()
    barrier = pltpu.get_barrier_semaphore()
    for step in range(1, n_gx):
        pl.semaphore_signal(barrier, inc=1, device_id=(lax.rem(gx + step, n_gx), gy), device_id_type=MESH)
    for step in range(1, n_gy):
        pl.semaphore_signal(barrier, inc=1, device_id=(gx, lax.rem(gy + step, n_gy)), device_id_type=MESH)
    load_h.wait()
    load_basis = pltpu.make_async_copy(basis_any.at[0, 0], basis, in_sem.at[1])
    load_basis.start()

    rows_of = lax.broadcasted_iota(jnp.int32, (B, B), 0)
    columns_of = lax.broadcasted_iota(jnp.int32, (B, B), 1)
    eye = rows_of == columns_of
    for code in range(9):
        block = h_buf[code]
        if code == 4:
            block = block + jnp.where(eye, onsite_ref[0], 0.0)
        else:
            block = block * pattern_ref[0, 0, code].astype(F32)
        high, low = split(block)
        hood[4, code // 3, code % 3, 0] = high
        hood[4, code // 3, code % 3, 1] = low
    pl.semaphore_wait(barrier, n_gx + n_gy - 2)

    copies = exchange(hood, sends, recvs, 0, gx, gy, n_gx, n_gy)
    begin(copies)
    for row in (1, 0, 2):
        forward(copies, row)
    for key in copies:
        if key in (BELOW_X, ABOVE_X) or key[0] not in (BELOW_Y, ABOVE_Y):
            copies[key].wait_recv()

    codes = [code_ref[0, 0, a] for a in range(SLOTS)]
    used = [code < 9 for code in codes]
    safe = [jnp.where(u, code, 4) for u, code in zip(used, codes)]
    off_x = [lax.div(s, 3) - 1 for s in safe]
    off_y = [lax.rem(s, 3) - 1 for s in safe]

    def stored(a, b):
        dx, dy = off_x[a] - off_x[b], off_y[a] - off_y[b]
        valid = (jnp.abs(dx) <= 1) & (jnp.abs(dy) <= 1) & used[a] & used[b]
        source = jnp.where(valid, safe[b], 4)
        row = jnp.where(valid, dx + 1, 1)
        col = jnp.where(valid, dy + 1, 1)
        block = hood[source, row, col, 0].astype(F32) + hood[source, row, col, 1].astype(F32)
        return jnp.where(valid, block, 0.0)

    def put(a, b, block):
        place = (slice(a * B, a * B + B), slice(b * B, b * B + B))
        m_f[place] = block
        high, low = split(block)
        m_hi[place] = high
        m_lo[place] = low

    for a in range(SLOTS):
        block = stored(a, a)
        put(a, a, 0.5 * (block + block.T))
        for b in range(a + 1, SLOTS):
            upper = 0.5 * (stored(a, b) + stored(b, a).T)
            put(a, b, upper)
            put(b, a, upper.T)

    def from_rows(vector):
        out = []
        for b in range(SLOTS):
            total = jnp.zeros((8, B), F32)
            for a in range(SLOTS):
                part = m_f[a * B:a * B + B, b * B:b * B + B] * vector[a]
                total = total + jnp.sum(part.reshape(B // 8, 8, B), axis=0)
            out.append(jnp.sum(total, axis=0, keepdims=True))
        return out

    def from_lanes(vector):
        out = []
        for a in range(SLOTS):
            total = jnp.zeros((B, B), F32)
            for b in range(SLOTS):
                total = total + m_f[a * B:a * B + B, b * B:b * B + B] * vector[b]
            out.append(jnp.sum(total, axis=1, keepdims=True))
        return out

    def norm2(vector):
        total = sum(part * part for part in vector)
        return jnp.sum(total, keepdims=True) + 1e-6

    vector = [jnp.full((B, 1), 1.0, F32) * u.astype(F32) for u in used]
    for step in range(POWER_STEPS + 1):
        image = from_rows(vector) if step % 2 == 0 else from_lanes(vector)
        squares = norm2(image)
        if step < POWER_STEPS:
            factor = lax.rsqrt(squares)
            vector = [part * factor for part in image]
    estimate = jnp.sqrt(squares)
    best[0] = jnp.broadcast_to(estimate, (8, B))

    def share(source, target, sends_to, recvs_to, count, axis):
        out = []
        for step in range(1, count):
            peer = (lax.rem(gx + step, n_gx), gy) if axis == 0 else (gx, lax.rem(gy + step, n_gy))
            out.append(pltpu.make_async_remote_copy(
                src_ref=best.at[source],
                dst_ref=target.at[step - 1],
                send_sem=sends_to.at[step - 1],
                recv_sem=recvs_to.at[step - 1],
                device_id=peer,
                device_id_type=MESH,
            ))
        return out

    along_x = share(0, best_x, sends_x, recvs_x, n_gx, 0)
    along_y = share(1, best_y, sends_y, recvs_y, n_gy, 1)
    for copy in along_x:
        copy.start()

    for r in range(0, ORDER, 256):
        for c in range(0, ORDER, 256):
            rows, cols = slice(r, r + 256), slice(c, c + 256)
            block = three((m_hi[rows, :], m_lo[rows, :]), (m_hi[:, cols], m_lo[:, cols]))
            high, low = split(block)
            q_hi[rows, cols] = high
            q_lo[rows, cols] = low

    top = best[0]
    for step, copy in enumerate(along_x):
        copy.wait_recv()
        top = jnp.maximum(top, best_x[step])
    best[1] = top
    for copy in along_y:
        copy.start()

    for r in range(0, ORDER, 256):
        for c in range(0, ORDER, 256):
            rows, cols = slice(r, r + 256), slice(c, c + 256)
            n_f[rows, cols] = three((m_hi[rows, :], m_lo[rows, :]), (q_hi[:, cols], q_lo[:, cols]))

    powers = [m_f[:, :B], n_f[:, :B]]
    for _ in range(3):
        powers.append(thin((q_hi, q_lo), *split(powers[-1])))

    top = best[1]
    for step, copy in enumerate(along_y):
        copy.wait_recv()
        top = jnp.maximum(top, best_y[step])
    inverse = 1.0 / (1.25 * top[:1, :1])
    square = inverse * inverse

    alpha, beta = 1.5 * inverse, -0.5 * inverse * square
    for r in range(0, ORDER, B):
        rows = slice(r, r + B)
        high, low = split(alpha * m_f[rows, :] + beta * n_f[rows, :])
        x_hi[rows, :] = high
        x_lo[rows, :] = low
    weights = (
        2.25 * inverse,
        inverse * square * (-0.75 - 0.5 * 3.375),
        inverse * square * square * (0.5 * 3.375),
        inverse * square * square * square * (-0.5 * 1.125),
        inverse * square * square * square * square * (0.5 * 0.125),
    )
    second = sum(w * p for w, p in zip(weights, powers))

    def applied(value):
        once = thin((x_hi, x_lo), *split(value))
        twice = thin((x_hi, x_lo), *split(once))
        return 1.5 * once - 0.5 * thin((x_hi, x_lo), *split(twice))

    third = 1.5 * second - 0.5 * applied(applied(second))
    for a in range(SLOTS):
        block = -third[a * B:a * B + B]
        if a == 0:
            block = jnp.where(eye, 1.0, 0.0) + block
        halves[a] = (0.5 * block).astype(BF16)
    for code in range(9):
        slot = jnp.int32(0)
        held = codes[0] == code
        for a in range(1, SLOTS):
            slot = jnp.where(codes[a] == code, a, slot)
            held = held | (codes[a] == code)
        block = jnp.where(held, halves[slot], jnp.zeros((B, B), BF16))
        dhood[4, code // 3, code % 3] = block
        density_ref[0, 0, code] = block

    dcopies = exchange(dhood, sends, recvs, COPIES + 2, gx, gy, n_gx, n_gy)
    begin(dcopies)
    load_basis.wait()

    def tile(place, first):
        near_x, near_y = place // 3 - 1, place % 3 - 1
        lefts, rights = [], []
        for code in range(9):
            far_x, far_y = near_x + code // 3 - 1, near_y + code % 3 - 1
            if abs(far_x) <= 1 and abs(far_y) <= 1:
                lefts.append((far_x + 1) * 3 + far_y + 1)
                rights.append(dhood[place, code // 3, code % 3])
        right = jnp.concatenate(rights, axis=0)
        for start in range(0, grid_acc.shape[0], 256):
            rows = slice(start, start + 256)
            left = jnp.concatenate([basis[e, rows, :] for e in lefts], axis=1)
            product = jnp.dot(left, right, preferred_element_type=F32)
            product = product * basis[place, rows, :].astype(F32)
            if first:
                grid_acc[rows, :] = product
            else:
                grid_acc[rows, :] = grid_acc[rows, :] + product

    tile(4, True)
    for row in (1, 0, 2):
        forward(dcopies, row)
    for place in (BELOW_Y, ABOVE_Y):
        tile(place, False)
    for place in (BELOW_X, ABOVE_X):
        dcopies[place].wait_recv()
        tile(place, False)
    for place in (0, 2, 6, 8):
        for row in range(3):
            if (place, row) in dcopies:
                dcopies[place, row].wait_recv()
        tile(place, False)
    for part in range(grid_acc.shape[0] // B):
        block = grid_acc[part * B:part * B + B, :]
        grid_ref[0, 0, pl.ds(part * B, B)] = jnp.sum(block.T, axis=0)

    for group in (copies, dcopies):
        for key in group:
            group[key].wait_send()
    for copy in along_x + along_y:
        copy.wait_send()


def local(n_gx, n_gy, hblocks, onsite, pattern, slot_code, basis):
    points = basis.shape[3]
    total = COPIES + 2
    any_space = pl.BlockSpec(memory_space=pl.ANY)
    vmem = pl.BlockSpec(memory_space=pltpu.VMEM)
    smem = pl.BlockSpec(memory_space=pltpu.SMEM)
    square = (ORDER, ORDER)
    return pl.pallas_call(
        functools.partial(kernel, n_gx, n_gy),
        out_shape=(
            jax.ShapeDtypeStruct((1, 1, 9, B, B), BF16),
            jax.ShapeDtypeStruct((1, 1, points), F32),
        ),
        in_specs=[any_space, vmem, smem, smem, any_space],
        out_specs=(vmem, vmem),
        scratch_shapes=[
            pltpu.VMEM((9, B, B), F32),
            pltpu.VMEM((9, points, B), BF16),
            pltpu.VMEM((9, 3, 3, 2, B, B), BF16),
            pltpu.VMEM(square, F32),
            pltpu.VMEM(square, BF16),
            pltpu.VMEM(square, BF16),
            pltpu.VMEM(square, BF16),
            pltpu.VMEM(square, BF16),
            pltpu.VMEM(square, F32),
            pltpu.VMEM(square, BF16),
            pltpu.VMEM(square, BF16),
            pltpu.VMEM((SLOTS, B, B), F32),
            pltpu.VMEM((SLOTS, B, B), BF16),
            pltpu.VMEM((9, 3, 3, B, B), BF16),
            pltpu.VMEM((points, B), F32),
            pltpu.VMEM((2, 8, B), F32),
            pltpu.VMEM((n_gx - 1, 8, B), F32),
            pltpu.VMEM((n_gy - 1, 8, B), F32),
            pltpu.SemaphoreType.DMA((2,)),
            pltpu.SemaphoreType.DMA((2 * total,)),
            pltpu.SemaphoreType.DMA((2 * total,)),
            pltpu.SemaphoreType.DMA((n_gx - 1,)),
            pltpu.SemaphoreType.DMA((n_gx - 1,)),
            pltpu.SemaphoreType.DMA((n_gy - 1,)),
            pltpu.SemaphoreType.DMA((n_gy - 1,)),
        ],
        compiler_params=pltpu.CompilerParams(
            collective_id=0, has_side_effects=True, vmem_limit_bytes=60 << 20
        ),
    )(hblocks, onsite, pattern, slot_code, basis)


def solution(mesh):
    placed = (
        P("gx", "gy", None, None, None),
        P("gx", "gy", None),
        P("gx", "gy", None),
        P("gx", "gy", None),
        P("gx", "gy", None, None, None),
    )
    return jax.shard_map(
        functools.partial(local, mesh.shape["gx"], mesh.shape["gy"]),
        mesh=mesh,
        in_specs=placed,
        out_specs=(P("gx", "gy", None, None, None), P("gx", "gy", None)),
        check_vma=False,
    )
```

profile of v0, /device:TPU:1, one launch (start us, length us, event | category | flops | bytes accessed | tf_op | source)
XLA Modules:
  0.0 57.3 jit_solution(10067152238660981369)
XLA Ops:
  0.6 53.7 %shard_map.68 = (bf16[1,1,9,128,128]{4,3,2,1,0:T(8,128)(2,1)}, f32[1,1,1024]{2,1,0:T(1,128)}) custom-call(f32[1,1,9,128,128]{4,3,2,1,0:T(8,128)} %h_any.1, f32[1,1,128]{2,1,0:T(1,128)} %onsite_ref.1, s32[1,1,9]{2,1,0:T(1,128)} %pattern_ref.1, s32[1,1,6]{2,1,0:T(1,128)} %code_ref.1, bf16[1,1,9,1024,128]{4,3,2,1,0:T(8,128)(2,1)} %basis_any.1), custom_call_target="tpu_custom_call" | custom-call | tf_op jit(solution)/shard_map/pallas_call | solution.py:354
  54.3 1.7 %copy.9 = bf16[1,1,9,128,128]{4,3,2,1,0:T(8,128)(2,1)} copy(bf16[1,1,9,128,128]{4,3,2,1,0:T(8,128)(2,1)} %get-tuple-element.4) | data formatting | bytes 589824
  56.0 1.3 %copy.10 = f32[1,1,1024]{2,1,0:T(1,128)} copy(f32[1,1,1024]{2,1,0:T(1,128)} %get-tuple-element.5) | data formatting | bytes 8192
where the time goes:
time: 57.5 us; the launch traced here: 57.3 us
  Pallas kernels  53.7 us (93%)
  local copies, waits for them, and re-layouts  2.97 us (5%)
  between operations  0.64 us (1%)
    pallas_call x1, Pallas kernels, local(): pl.pallas_call(functools.partial(kernel, n_gx, n_gy), out_shape=(jax.Shap...  53.7 us
    unnamed x2, local copies, waits for them, and re-layouts  2.97 us

commit v1 on v0

--- a/solution.py
+++ b/solution.py
@@ -16,11 +16,10 @@
 BF16 = jnp.bfloat16
 
 BELOW_X, ABOVE_X, BELOW_Y, ABOVE_Y = 1, 7, 3, 5
-
-
-def needed(place):
-    spans = (slice(1, 3), slice(0, 3), slice(0, 2))
-    return spans[place // 3], spans[place % 3]
+COPIES = 18
+
+HIGH = 1
+LOW = (0, 5, 4)
 
 
 def split(value):
@@ -28,63 +27,97 @@
     return high, (value - high.astype(F32)).astype(BF16)
 
 
-def exchange(hood, sends, recvs, base, gx, gy, n_gx, n_gy):
-    up_x = (lax.rem(gx + 1, n_gx), gy)
-    down_x = (lax.rem(gx + n_gx - 1, n_gx), gy)
-    up_y = (gx, lax.rem(gy + 1, n_gy))
-    down_y = (gx, lax.rem(gy + n_gy - 1, n_gy))
-
-    def copy(index, source, target, rows, columns, device):
-        return pltpu.make_async_remote_copy(
-            src_ref=hood.at[source, rows, columns],
-            dst_ref=hood.at[target, rows, columns],
-            send_sem=sends.at[index],
-            recv_sem=recvs.at[index],
-            device_id=device,
-            device_id_type=MESH,
-        )
-
-    copies = {}
-    index = base
-    for row in (1, 0, 2):
-        for place, device in ((BELOW_Y, up_y), (ABOVE_Y, down_y)):
-            columns = needed(place)[1]
-            copies[place, row] = copy(index, 4, place, slice(row, row + 1), columns, device)
-            index += 1
-    for place, device in ((BELOW_X, up_x), (ABOVE_X, down_x)):
-        rows, columns = needed(place)
-        copies[place] = copy(index, 4, place, rows, columns, device)
-        index += 1
-    for row in (1, 0, 2):
-        for source in (BELOW_Y, ABOVE_Y):
-            for shift, device in ((-1, up_x), (1, down_x)):
-                place = source + 3 * shift
-                rows, columns = needed(place)
-                if rows.start <= row < rows.stop:
-                    copies[place, row] = copy(
-                        index, source, place, slice(row, row + 1), columns, device
-                    )
-                    index += 1
-    return copies
-
-
-COPIES = 16
-
-
-def begin(copies):
-    for row in (1, 0, 2):
-        for place in (BELOW_Y, ABOVE_Y):
-            copies[place, row].start()
-    for place in (BELOW_X, ABOVE_X):
-        copies[place].start()
-
-
-def forward(copies, row):
-    for source in (BELOW_Y, ABOVE_Y):
-        copies[source, row].wait_recv()
-        for place in (source - 3, source + 3):
-            if (place, row) in copies:
-                copies[place, row].start()
+class Exchange:
+    def __init__(self, hood, sends, recvs, base, gx, gy, n_gx, n_gy, lows):
+        odd = lax.rem(gx, 2)
+        up_y = (gx, lax.rem(gy + 1, n_gy))
+        down_y = (gx, lax.rem(gy + n_gy - 1, n_gy))
+        step = 2 * odd - 1
+        far = (lax.rem(gx + step + n_gx, n_gx), gy)
+        near = (gx - step, gy)
+        self.index = base
+
+        def copy(source, target, rows, columns, device):
+            index = self.index
+            self.index += 1
+            return pltpu.make_async_remote_copy(
+                src_ref=hood.at[source, rows, columns],
+                dst_ref=hood.at[target, rows, columns],
+                send_sem=sends.at[index],
+                recv_sem=recvs.at[index],
+                device_id=device,
+                device_id_type=MESH,
+            )
+
+        if lows:
+            wide = {BELOW_Y: slice(2, 5), ABOVE_Y: slice(0, 3)}
+            slim = {BELOW_Y: slice(2, 4), ABOVE_Y: slice(1, 3)}
+            across = slice(1, 4)
+        else:
+            wide = slim = {BELOW_Y: slice(1, 3), ABOVE_Y: slice(0, 2)}
+            across = slice(0, 3)
+        towards_far = pl.ds(2 * odd, 1)
+        towards_near = pl.ds(2 - 2 * odd, 1)
+        middle = pl.ds(1, 1)
+        self.along_y = []
+        self.onward = []
+        sides = ((BELOW_Y, up_y), (ABOVE_Y, down_y))
+        for rows in (middle, towards_far, towards_near):
+            self.along_y.append([copy(4, place, rows, wide[place], device) for place, device in sides])
+        self.along_x = [
+            copy(4, 4 - 3 * step, pl.ds(odd, 2), across, far),
+            copy(4, 4 + 3 * step, pl.ds(1 - odd, 2), across, near),
+        ]
+        if lows:
+            single = slice(LOW[1], LOW[1] + 1)
+            self.along_x += [
+                copy(4, 4 - 3 * step, towards_far, single, far),
+                copy(4, 4 + 3 * step, towards_near, single, near),
+            ]
+        for rows, columns, targets in (
+            (middle, slim, ((far, -3 * step), (near, 3 * step))),
+            (towards_far, wide, ((far, -3 * step),)),
+            (towards_near, wide, ((near, 3 * step),)),
+        ):
+            self.onward.append([
+                [copy(source, source + shift, rows, columns[source], device) for device, shift in targets]
+                for source in (BELOW_Y, ABOVE_Y)
+            ])
+
+    def begin_row(self, order):
+        for copy in self.along_y[order]:
+            copy.start()
+
+    def begin_x(self):
+        for copy in self.along_x:
+            copy.start()
+
+    def forward(self, order):
+        for arriving, going in zip(self.along_y[order], self.onward[order]):
+            arriving.wait_recv()
+            for copy in going:
+                copy.start()
+
+    def wait_x(self):
+        for copy in self.along_x:
+            copy.wait_recv()
+
+    def wait_onward(self):
+        for order in self.onward:
+            for going in order:
+                for copy in going:
+                    copy.wait_recv()
+
+    def wait_sent(self):
+        for group in self.along_y:
+            for copy in group:
+                copy.wait_send()
+        for copy in self.along_x:
+            copy.wait_send()
+        for order in self.onward:
+            for going in order:
+                for copy in going:
+                    copy.wait_send()
 
 
 def three(left, right):
@@ -106,46 +139,69 @@
 
 def kernel(
     n_gx, n_gy,
-    h_any, onsite_ref, pattern_ref, code_ref, basis_any,
+    h_any, onsite_any, pattern_any, code_any, basis_any,
     density_ref, grid_ref,
-    h_buf, basis, hood, m_f, m_hi, m_lo, q_hi, q_lo, n_f, x_hi, x_lo,
-    column, halves, dhood, grid_acc, best, best_x, best_y,
+    h_buf, onsite_ref, pattern_ref, code_ref, basis, hood, m_f, m_hi, m_lo, q_hi, q_lo, n_f, x_hi, x_lo,
+    halves, dhood, grid_acc, best, best_x, best_y,
     in_sem, sends, recvs, sends_x, recvs_x, sends_y, recvs_y,
 ):
     gx, gy = lax.axis_index("gx"), lax.axis_index("gy")
 
-    load_h = pltpu.make_async_copy(h_any.at[0, 0], h_buf, in_sem.at[0])
-    load_h.start()
     barrier = pltpu.get_barrier_semaphore()
     for step in range(1, n_gx):
         pl.semaphore_signal(barrier, inc=1, device_id=(lax.rem(gx + step, n_gx), gy), device_id_type=MESH)
     for step in range(1, n_gy):
         pl.semaphore_signal(barrier, inc=1, device_id=(gx, lax.rem(gy + step, n_gy)), device_id_type=MESH)
-    load_h.wait()
-    load_basis = pltpu.make_async_copy(basis_any.at[0, 0], basis, in_sem.at[1])
+    loads = []
+    for order, row in enumerate((1, 0, 2)):
+        rows = pl.ds(3 * row, 3)
+        loads.append(pltpu.make_async_copy(h_any.at[0, 0, rows], h_buf.at[rows], in_sem.at[order]))
+        loads[-1].start()
+        if order == 0:
+            load_pattern = pltpu.make_async_copy(pattern_any, pattern_ref, in_sem.at[4])
+            load_onsite = pltpu.make_async_copy(onsite_any, onsite_ref, in_sem.at[5])
+            load_codes = pltpu.make_async_copy(code_any, code_ref, in_sem.at[6])
+            load_pattern.start()
+            load_onsite.start()
+            load_codes.start()
+    load_basis = pltpu.make_async_copy(basis_any.at[0, 0], basis, in_sem.at[3])
     load_basis.start()
 
     rows_of = lax.broadcasted_iota(jnp.int32, (B, B), 0)
     columns_of = lax.broadcasted_iota(jnp.int32, (B, B), 1)
     eye = rows_of == columns_of
-    for code in range(9):
-        block = h_buf[code]
-        if code == 4:
-            block = block + jnp.where(eye, onsite_ref[0], 0.0)
-        else:
-            block = block * pattern_ref[0, 0, code].astype(F32)
-        high, low = split(block)
-        hood[4, code // 3, code % 3, 0] = high
-        hood[4, code // 3, code % 3, 1] = low
+
+    def prepare(row):
+        for col in range(3):
+            code = 3 * row + col
+            block = h_buf[code]
+            if code == 4:
+                block = block + jnp.where(eye, onsite_ref[0], 0.0)
+            else:
+                block = block * pattern_ref[0, 0, code].astype(F32)
+            high, low = split(block)
+            hood[4, row, HIGH + col] = high
+            hood[4, row, LOW[col]] = low
+
+    swap = Exchange(hood, sends, recvs, 0, gx, gy, n_gx, n_gy, True)
+    load_pattern.wait()
+    load_onsite.wait()
+    load_codes.wait()
+    loads[0].wait()
+    prepare(1)
     pl.semaphore_wait(barrier, n_gx + n_gy - 2)
-
-    copies = exchange(hood, sends, recvs, 0, gx, gy, n_gx, n_gy)
-    begin(copies)
-    for row in (1, 0, 2):
-        forward(copies, row)
-    for key in copies:
-        if key in (BELOW_X, ABOVE_X) or key[0] not in (BELOW_Y, ABOVE_Y):
-            copies[key].wait_recv()
+    swap.begin_row(0)
+    loads[1].wait()
+    prepare(0)
+    loads[2].wait()
+    prepare(2)
+    swap.begin_row(1)
+    swap.begin_row(2)
+    swap.begin_x()
+    for order in range(3):
+        swap.forward(order)
+    swap.wait_x()
+    swap.wait_onward()
 
     codes = [code_ref[0, 0, a] for a in range(SLOTS)]
     used = [code < 9 for code in codes]
@@ -159,7 +215,10 @@
         source = jnp.where(valid, safe[b], 4)
         row = jnp.where(valid, dx + 1, 1)
         col = jnp.where(valid, dy + 1, 1)
-        block = hood[source, row, col, 0].astype(F32) + hood[source, row, col, 1].astype(F32)
+        block = hood[source, row, col + HIGH].astype(F32)
+        if a == 0 or b == 0:
+            plane = jnp.where(col == 1, LOW[1], jnp.where(col == 0, LOW[0], LOW[2]))
+            block = block + hood[source, row, plane].astype(F32)
         return jnp.where(valid, block, 0.0)
 
     def put(a, b, block):
@@ -230,12 +289,16 @@
         copy.start()
 
     for r in range(0, ORDER, 256):
-        for c in range(0, ORDER, 256):
+        for c in range(r, ORDER, 256):
             rows, cols = slice(r, r + 256), slice(c, c + 256)
             block = three((m_hi[rows, :], m_lo[rows, :]), (m_hi[:, cols], m_lo[:, cols]))
             high, low = split(block)
             q_hi[rows, cols] = high
             q_lo[rows, cols] = low
+            if r != c:
+                high, low = split(block.T)
+                q_hi[cols, rows] = high
+                q_lo[cols, rows] = low
 
     top = best[0]
     for step, copy in enumerate(along_x):
@@ -246,9 +309,12 @@
         copy.start()
 
     for r in range(0, ORDER, 256):
-        for c in range(0, ORDER, 256):
+        for c in range(r, ORDER, 256):
             rows, cols = slice(r, r + 256), slice(c, c + 256)
-            n_f[rows, cols] = three((m_hi[rows, :], m_lo[rows, :]), (q_hi[:, cols], q_lo[:, cols]))
+            block = three((m_hi[rows, :], m_lo[rows, :]), (q_hi[:, cols], q_lo[:, cols]))
+            n_f[rows, cols] = block
+            if r != c:
+                n_f[cols, rows] = block.T
 
     powers = [m_f[:, :B], n_f[:, :B]]
     for _ in range(3):
@@ -286,19 +352,20 @@
         block = -third[a * B:a * B + B]
         if a == 0:
             block = jnp.where(eye, 1.0, 0.0) + block
-        halves[a] = (0.5 * block).astype(BF16)
+        halves[a] = 0.5 * block
+    share_out = Exchange(dhood, sends, recvs, COPIES, gx, gy, n_gx, n_gy, False)
     for code in range(9):
         slot = jnp.int32(0)
         held = codes[0] == code
         for a in range(1, SLOTS):
             slot = jnp.where(codes[a] == code, a, slot)
             held = held | (codes[a] == code)
-        block = jnp.where(held, halves[slot], jnp.zeros((B, B), BF16))
-        dhood[4, code // 3, code % 3] = block
+        block = jnp.where(held, halves[slot], 0.0)
+        dhood[4, code // 3, code % 3] = block.astype(BF16)
         density_ref[0, 0, code] = block
-
-    dcopies = exchange(dhood, sends, recvs, COPIES + 2, gx, gy, n_gx, n_gy)
-    begin(dcopies)
+    for order in range(3):
+        share_out.begin_row(order)
+    share_out.begin_x()
     load_basis.wait()
 
     def tile(place, first):
@@ -321,48 +388,52 @@
                 grid_acc[rows, :] = grid_acc[rows, :] + product
 
     tile(4, True)
-    for row in (1, 0, 2):
-        forward(dcopies, row)
-    for place in (BELOW_Y, ABOVE_Y):
-        tile(place, False)
-    for place in (BELOW_X, ABOVE_X):
-        dcopies[place].wait_recv()
-        tile(place, False)
+    share_out.forward(0)
+    share_out.forward(1)
+    share_out.wait_x()
+    tile(BELOW_X, False)
+    share_out.forward(2)
+    tile(ABOVE_X, False)
+    tile(BELOW_Y, False)
+    tile(ABOVE_Y, False)
+    share_out.wait_onward()
     for place in (0, 2, 6, 8):
-        for row in range(3):
-            if (place, row) in dcopies:
-                dcopies[place, row].wait_recv()
         tile(place, False)
     for part in range(grid_acc.shape[0] // B):
-        block = grid_acc[part * B:part * B + B, :]
-        grid_ref[0, 0, pl.ds(part * B, B)] = jnp.sum(block.T, axis=0)
-
-    for group in (copies, dcopies):
-        for key in group:
-            group[key].wait_send()
+        block = grid_acc[part * B:part * B + B, :].T
+        grid_ref[:, part * B:part * B + B] = jnp.sum(block.reshape(B // 8, 8, B), axis=0)
+
+    swap.wait_sent()
+    share_out.wait_sent()
     for copy in along_x + along_y:
         copy.wait_send()
 
 
 def local(n_gx, n_gy, hblocks, onsite, pattern, slot_code, basis):
     points = basis.shape[3]
-    total = COPIES + 2
-    any_space = pl.BlockSpec(memory_space=pl.ANY)
+    total = COPIES
+    hbm = pl.BlockSpec(memory_space=pltpu.HBM)
     vmem = pl.BlockSpec(memory_space=pltpu.VMEM)
-    smem = pl.BlockSpec(memory_space=pltpu.SMEM)
     square = (ORDER, ORDER)
-    return pl.pallas_call(
+    hblocks, onsite, pattern, slot_code, basis = [
+        pltpu.with_memory_space_constraint(x, pltpu.HBM)
+        for x in (hblocks, onsite, pattern, slot_code, basis)
+    ]
+    density, grid = pl.pallas_call(
         functools.partial(kernel, n_gx, n_gy),
         out_shape=(
-            jax.ShapeDtypeStruct((1, 1, 9, B, B), BF16),
-            jax.ShapeDtypeStruct((1, 1, points), F32),
+            jax.ShapeDtypeStruct((1, 1, 9, B, B), F32),
+            jax.ShapeDtypeStruct((8, points), F32),
         ),
-        in_specs=[any_space, vmem, smem, smem, any_space],
+        in_specs=[hbm] * 5,
         out_specs=(vmem, vmem),
         scratch_shapes=[
             pltpu.VMEM((9, B, B), F32),
+            pltpu.VMEM((1, 1, B), F32),
+            pltpu.SMEM((1, 1, 9), jnp.int32),
+            pltpu.SMEM((1, 1, SLOTS), jnp.int32),
             pltpu.VMEM((9, points, B), BF16),
-            pltpu.VMEM((9, 3, 3, 2, B, B), BF16),
+            pltpu.VMEM((9, 3, 6, B, B), BF16),
             pltpu.VMEM(square, F32),
             pltpu.VMEM(square, BF16),
             pltpu.VMEM(square, BF16),
@@ -372,13 +443,12 @@
             pltpu.VMEM(square, BF16),
             pltpu.VMEM(square, BF16),
             pltpu.VMEM((SLOTS, B, B), F32),
-            pltpu.VMEM((SLOTS, B, B), BF16),
             pltpu.VMEM((9, 3, 3, B, B), BF16),
             pltpu.VMEM((points, B), F32),
             pltpu.VMEM((2, 8, B), F32),
             pltpu.VMEM((n_gx - 1, 8, B), F32),
             pltpu.VMEM((n_gy - 1, 8, B), F32),
-            pltpu.SemaphoreType.DMA((2,)),
+            pltpu.SemaphoreType.DMA((7,)),
             pltpu.SemaphoreType.DMA((2 * total,)),
             pltpu.SemaphoreType.DMA((2 * total,)),
             pltpu.SemaphoreType.DMA((n_gx - 1,)),
@@ -387,9 +457,10 @@
             pltpu.SemaphoreType.DMA((n_gy - 1,)),
         ],
         compiler_params=pltpu.CompilerParams(
-            collective_id=0, has_side_effects=True, vmem_limit_bytes=60 << 20
+            collective_id=0, has_side_effects=True, vmem_limit_bytes=40 << 20
         ),
     )(hblocks, onsite, pattern, slot_code, basis)
+    return density.astype(BF16), jnp.sum(grid, axis=0)[None, None]
 
 
 def solution(mesh):

time: 57.5 us -> 51.1 us (0.89)
  Pallas kernels: 53.7 us -> 49 us
  local copies, waits for them, and re-layouts: 2.97 us -> 0 us
  other arithmetic: 0 us -> 1.37 us
    pallas_call x1, Pallas kernels: 53.7 us -> 49 us  [local(): pl.pallas_call(functools.partial(kernel, n_gx, n_gy), out_shape=(jax.Shap...]
    unnamed x2 -> x0, local copies, waits for them, and re-layouts: 2.97 us -> none
    convert_element_type x0 -> x1, other arithmetic: none -> 0.76 us  [local(): return (density.astype(BF16), jnp.sum(grid, axis=0)[None, None])]
    reduce_sum x0 -> x1, other arithmetic: none -> 0.6 us  [local(): return (density.astype(BF16), jnp.sum(grid, axis=0)[None, None])]
where the time goes in v1:
time: 51.1 us; the launch traced here: 51 us
  Pallas kernels  49 us (96%)
  other arithmetic  1.37 us (3%)
  between operations  0.64 us (1%)
    pallas_call x1, Pallas kernels, local(): pl.pallas_call(functools.partial(kernel, n_gx, n_gy), out_shape=(jax.Shap...  49 us

profile of v1, /device:TPU:1, one launch (start us, length us, event | category | flops | bytes accessed | tf_op | source)
XLA Modules:
  0.0 51.0 jit_solution(2190595265366853224)
XLA Ops:
  0.6 49.0 %shard_map.68 = (f32[1,1,9,128,128]{4,3,2,1,0:T(8,128)S(1)}, f32[8,1024]{1,0:T(8,128)S(1)}) custom-call(f32[1,1,9,128,128]{4,3,2,1,0:T(8,128)} %h_any.1, f32[1,1,128]{2,1,0:T(1,128)} %onsite_any.1, s32[1,1,9]{2,1,0:T(1,128)} %pattern_any.1, s32[1,1,6]{2,1,0:T(1,128)} %code_any.1, bf16[1,1,9,1024,128]{4,3,2,1,0:T(8,128)(2,1)} %basis_any.1), custom_call_target="tpu_custom_call" | custom-call | tf_op jit(solution)/shard_map/pallas_call | solution.py:422
  49.6 0.8 %convert_element_type.3 = bf16[1,1,9,128,128]{4,3,2,1,0:T(8,128)(2,1)} convert(f32[1,1,9,128,128]{4,3,2,1,0:T(8,128)S(1)} %get-tuple-element.4) | non-fusion elementwise | flops 147456 | bytes 884736 | tf_op jit(solution)/shard_map/convert_element_type | solution.py:463
  50.4 0.6 %reduce_sum.9 = f32[1024]{0:T(1024)} reduce(f32[8,1024]{1,0:T(8,128)S(1)} %get-tuple-element.5, f32[]{:T(128)} %constant.0.clone.1), dimensions={0}, to_apply=%region_0.0 | reduce | flops 7168 | bytes 36868 | tf_op jit(solution)/shard_map/reduce_sum | solution.py:463

commit v2 on v1

--- a/solution.py
+++ b/solution.py
@@ -16,7 +16,7 @@
 BF16 = jnp.bfloat16
 
 BELOW_X, ABOVE_X, BELOW_Y, ABOVE_Y = 1, 7, 3, 5
-COPIES = 18
+COPIES = 18 + 14 + 10
 
 HIGH = 1
 LOW = (0, 5, 4)
@@ -49,21 +49,38 @@
                 device_id_type=MESH,
             )
 
-        if lows:
-            wide = {BELOW_Y: slice(2, 5), ABOVE_Y: slice(0, 3)}
-            slim = {BELOW_Y: slice(2, 4), ABOVE_Y: slice(1, 3)}
-            across = slice(1, 4)
-        else:
-            wide = slim = {BELOW_Y: slice(1, 3), ABOVE_Y: slice(0, 2)}
-            across = slice(0, 3)
+        def planes(place, low):
+            if not lows:
+                return (1, 2) if place == BELOW_Y else (0, 1)
+            if place == BELOW_Y:
+                return (2, 3, 4) if low else (2, 3)
+            return (1, 2, 0) if low else (1, 2)
+
         towards_far = pl.ds(2 * odd, 1)
         towards_near = pl.ds(2 - 2 * odd, 1)
         middle = pl.ds(1, 1)
-        self.along_y = []
-        self.onward = []
+        to_far, to_near = (far, -3 * step), (near, 3 * step)
         sides = ((BELOW_Y, up_y), (ABOVE_Y, down_y))
-        for rows in (middle, towards_far, towards_near):
-            self.along_y.append([copy(4, place, rows, wide[place], device) for place, device in sides])
+        self.steps = []
+
+        def add(rows, targets, low, only_low=False):
+            for which in range(3 if lows else 2):
+                is_low = which == 2
+                if is_low and not low or only_low and not is_low:
+                    continue
+                for place, device in sides:
+                    plane = planes(place, True)[which]
+                    columns = slice(plane, plane + 1)
+                    arriving = copy(4, place, rows, columns, device)
+                    going = [copy(place, place + shift, rows, columns, peer) for peer, shift in targets]
+                    self.steps.append((arriving, going))
+
+        add(middle, (to_far, to_near), False)
+        add(towards_far, (to_far,), lows)
+        add(towards_near, (to_near,), lows)
+        if lows:
+            add(middle, (), True, True)
+        across = slice(1, 4) if lows else slice(0, 3)
         self.along_x = [
             copy(4, 4 - 3 * step, pl.ds(odd, 2), across, far),
             copy(4, 4 + 3 * step, pl.ds(1 - odd, 2), across, near),
@@ -74,50 +91,34 @@
                 copy(4, 4 - 3 * step, towards_far, single, far),
                 copy(4, 4 + 3 * step, towards_near, single, near),
             ]
-        for rows, columns, targets in (
-            (middle, slim, ((far, -3 * step), (near, 3 * step))),
-            (towards_far, wide, ((far, -3 * step),)),
-            (towards_near, wide, ((near, 3 * step),)),
-        ):
-            self.onward.append([
-                [copy(source, source + shift, rows, columns[source], device) for device, shift in targets]
-                for source in (BELOW_Y, ABOVE_Y)
-            ])
-
-    def begin_row(self, order):
-        for copy in self.along_y[order]:
-            copy.start()
+        self.to_far = [c for n, (_, copies) in enumerate(self.steps) for c in copies[:1] if n < (10 if lows else 8)]
+        self.to_near = [c for n, (_, copies) in enumerate(self.steps) for c in copies[-1:] if n < 4 or n >= (10 if lows else 8)]
+
+    def begin(self, first, last):
+        for arriving, _ in self.steps[first:last]:
+            arriving.start()
 
     def begin_x(self):
         for copy in self.along_x:
             copy.start()
 
-    def forward(self, order):
-        for arriving, going in zip(self.along_y[order], self.onward[order]):
+    def forward(self, first, last):
+        for arriving, going in self.steps[first:last]:
             arriving.wait_recv()
             for copy in going:
                 copy.start()
 
-    def wait_x(self):
-        for copy in self.along_x:
+    def wait(self, copies):
+        for copy in copies:
             copy.wait_recv()
 
-    def wait_onward(self):
-        for order in self.onward:
-            for going in order:
-                for copy in going:
-                    copy.wait_recv()
-
     def wait_sent(self):
-        for group in self.along_y:
-            for copy in group:
+        for arriving, going in self.steps:
+            arriving.wait_send()
+            for copy in going:
                 copy.wait_send()
         for copy in self.along_x:
             copy.wait_send()
-        for order in self.onward:
-            for going in order:
-                for copy in going:
-                    copy.wait_send()
 
 
 def three(left, right):
@@ -190,18 +191,15 @@
     loads[0].wait()
     prepare(1)
     pl.semaphore_wait(barrier, n_gx + n_gy - 2)
-    swap.begin_row(0)
+    swap.begin(0, 4)
     loads[1].wait()
     prepare(0)
     loads[2].wait()
     prepare(2)
-    swap.begin_row(1)
-    swap.begin_row(2)
+    swap.begin(4, 18)
     swap.begin_x()
-    for order in range(3):
-        swap.forward(order)
-    swap.wait_x()
-    swap.wait_onward()
+    swap.forward(0, 18)
+    swap.wait(swap.along_x + swap.to_near + swap.to_far)
 
     codes = [code_ref[0, 0, a] for a in range(SLOTS)]
     used = [code < 9 for code in codes]
@@ -360,22 +358,30 @@
         for a in range(1, SLOTS):
             slot = jnp.where(codes[a] == code, a, slot)
             held = held | (codes[a] == code)
-        block = jnp.where(held, halves[slot], 0.0)
-        dhood[4, code // 3, code % 3] = block.astype(BF16)
+        block = jnp.where(held, halves[slot], 0.0).astype(BF16)
+        dhood[4, code // 3, code % 3] = block
         density_ref[0, 0, code] = block
-    for order in range(3):
-        share_out.begin_row(order)
+    share_out.begin(0, 12)
     share_out.begin_x()
     load_basis.wait()
 
-    def tile(place, first):
-        near_x, near_y = place // 3 - 1, place % 3 - 1
+    step = 2 * lax.rem(gx, 2) - 1
+
+    def tile(near_x, near_y, first=False):
+        fixed = isinstance(near_x, int)
+        place = (near_x + 1) * 3 + near_y + 1
+        if fixed:
+            firsts = range(max(-near_x, 0), 3 - max(near_x, 0))
+        else:
+            start = lax.div(1 - near_x, 2)
+            firsts = (start, start + 1)
         lefts, rights = [], []
-        for code in range(9):
-            far_x, far_y = near_x + code // 3 - 1, near_y + code % 3 - 1
-            if abs(far_x) <= 1 and abs(far_y) <= 1:
-                lefts.append((far_x + 1) * 3 + far_y + 1)
-                rights.append(dhood[place, code // 3, code % 3])
+        for row in firsts:
+            for col in range(3):
+                far_y = near_y + col - 1
+                if abs(far_y) <= 1:
+                    lefts.append((near_x + row) * 3 + far_y + 1)
+                    rights.append(dhood[place, row, col])
         right = jnp.concatenate(rights, axis=0)
         for start in range(0, grid_acc.shape[0], 256):
             rows = slice(start, start + 256)
@@ -387,26 +393,37 @@
             else:
                 grid_acc[rows, :] = grid_acc[rows, :] + product
 
-    tile(4, True)
-    share_out.forward(0)
-    share_out.forward(1)
-    share_out.wait_x()
-    tile(BELOW_X, False)
-    share_out.forward(2)
-    tile(ABOVE_X, False)
-    tile(BELOW_Y, False)
-    tile(ABOVE_Y, False)
-    share_out.wait_onward()
-    for place in (0, 2, 6, 8):
-        tile(place, False)
+    tile(0, 0, True)
+    share_out.forward(0, 8)
+    share_out.wait(share_out.along_x)
+    tile(-1, 0)
+    share_out.forward(8, 12)
+    tile(1, 0)
+    tile(0, -1)
+    tile(0, 1)
+    share_out.wait(share_out.to_near)
+    tile(-step, -1)
+    tile(-step, 1)
+    share_out.wait(share_out.to_far)
+    tile(step, -1)
+    tile(step, 1)
     for part in range(grid_acc.shape[0] // B):
         block = grid_acc[part * B:part * B + B, :].T
-        grid_ref[:, part * B:part * B + B] = jnp.sum(block.reshape(B // 8, 8, B), axis=0)
+        grid_ref[0, :, pl.ds(part * B, B)] = jnp.sum(block, axis=0, keepdims=True)
 
     swap.wait_sent()
     share_out.wait_sent()
     for copy in along_x + along_y:
         copy.wait_send()
+
+
+def write_out(density_in, grid_in, density_out, grid_out, sems):
+    first = pltpu.make_async_copy(density_in, density_out, sems.at[0])
+    second = pltpu.make_async_copy(grid_in, grid_out, sems.at[1])
+    first.start()
+    second.start()
+    first.wait()
+    second.wait()
 
 
 def local(n_gx, n_gy, hblocks, onsite, pattern, slot_code, basis):
@@ -422,8 +439,8 @@
     density, grid = pl.pallas_call(
         functools.partial(kernel, n_gx, n_gy),
         out_shape=(
-            jax.ShapeDtypeStruct((1, 1, 9, B, B), F32),
-            jax.ShapeDtypeStruct((8, points), F32),
+            jax.ShapeDtypeStruct((1, 1, 9, B, B), BF16),
+            jax.ShapeDtypeStruct((1, 1, points), F32),
         ),
         in_specs=[hbm] * 5,
         out_specs=(vmem, vmem),
@@ -460,7 +477,17 @@
             collective_id=0, has_side_effects=True, vmem_limit_bytes=40 << 20
         ),
     )(hblocks, onsite, pattern, slot_code, basis)
-    return density.astype(BF16), jnp.sum(grid, axis=0)[None, None]
+    space = pl.BlockSpec(memory_space=pl.ANY)
+    return pl.pallas_call(
+        write_out,
+        out_shape=(
+            jax.ShapeDtypeStruct(density.shape, BF16),
+            jax.ShapeDtypeStruct(grid.shape, F32),
+        ),
+        in_specs=[vmem, vmem],
+        out_specs=(space, space),
+        scratch_shapes=[pltpu.SemaphoreType.DMA((2,))],
+    )(*[pltpu.with_memory_space_constraint(x, pltpu.VMEM) for x in (density, grid)])
 
 
 def solution(mesh):

time: 51.1 us -> 48.4 us (0.947)
  Pallas kernels: 49 us -> 47.4 us
  other arithmetic: 1.37 us -> 0 us
    pallas_call x1, Pallas kernels: 49 us -> 46.7 us  [local(): pl.pallas_call(functools.partial(kernel, n_gx, n_gy), out_shape=(jax.Shap...]
    convert_element_type x1 -> x0, other arithmetic: 0.76 us -> none  [local(): return (density.astype(BF16), jnp.sum(grid, axis=0)[None, None])]
    pallas_call x0 -> x1, Pallas kernels: none -> 0.74 us  [local(): pl.pallas_call(write_out, out_shape=(jax.ShapeDtypeStruct(density.shape,...]
    reduce_sum x1 -> x0, other arithmetic: 0.6 us -> none  [local(): return (density.astype(BF16), jnp.sum(grid, axis=0)[None, None])]
where the time goes in v2:
time: 48.4 us; the launch traced here: 48.2 us
  Pallas kernels  47.4 us (98%)
  between operations  0.8 us (2%)
    pallas_call x1, Pallas kernels, local(): pl.pallas_call(functools.partial(kernel, n_gx, n_gy), out_shape=(jax.Shap...  46.7 us

profile of v2, /device:TPU:1, one launch (start us, length us, event | category | flops | bytes accessed | tf_op | source)
XLA Modules:
  0.0 48.2 jit_solution(5720853890838504957)
XLA Ops:
  0.6 46.7 %shard_map.68 = (bf16[1,1,9,128,128]{4,3,2,1,0:T(8,128)(2,1)S(1)}, f32[1,1,1024]{2,1,0:T(1,128)S(1)}) custom-call(f32[1,1,9,128,128]{4,3,2,1,0:T(8,128)} %h_any.1, f32[1,1,128]{2,1,0:T(1,128)} %onsite_any.1, s32[1,1,9]{2,1,0:T(1,128)} %pattern_any.1, s32[1,1,6]{2,1,0:T(1,128)} %code_any.1, bf16[1,1,9,1024,128]{4,3,2,1,0:T(8,128)(2,1)} %basis_any.1), custom_call_target="tpu_custom_call" | custom-call | tf_op jit(solution)/shard_map/pallas_call | solution.py:439
  47.3 0.7 %shard_map.69 = (bf16[1,1,9,128,128]{4,3,2,1,0:T(8,128)(2,1)}, f32[1,1,1024]{2,1,0:T(1,128)}) custom-call(bf16[1,1,9,128,128]{4,3,2,1,0:T(8,128)(2,1)S(1)} %get-tuple-element.4.density_in, f32[1,1,1024]{2,1,0:T(1,128)S(1)} %get-tuple-element.5.grid_in), custom_call_target="tpu_custom_call" | custom-call | tf_op jit(solution)/shard_map/pallas_call | solution.py:481

commit v3 on v2

--- a/solution.py
+++ b/solution.py
@@ -148,23 +148,25 @@
 ):
     gx, gy = lax.axis_index("gx"), lax.axis_index("gy")
 
+    small = [
+        pltpu.make_async_copy(source, target, in_sem.at[4 + n])
+        for n, (source, target) in enumerate((
+            (pattern_any, pattern_ref), (onsite_any, onsite_ref), (code_any, code_ref),
+        ))
+    ]
+    loads = []
+    for order, row in enumerate((1, 0, 2)):
+        rows = pl.ds(3 * row, 3)
+        loads.append(pltpu.make_async_copy(h_any.at[0, 0, rows], h_buf.at[rows], in_sem.at[order]))
+    for copy in [loads[0]] + small:
+        copy.start()
     barrier = pltpu.get_barrier_semaphore()
     for step in range(1, n_gx):
         pl.semaphore_signal(barrier, inc=1, device_id=(lax.rem(gx + step, n_gx), gy), device_id_type=MESH)
     for step in range(1, n_gy):
         pl.semaphore_signal(barrier, inc=1, device_id=(gx, lax.rem(gy + step, n_gy)), device_id_type=MESH)
-    loads = []
-    for order, row in enumerate((1, 0, 2)):
-        rows = pl.ds(3 * row, 3)
-        loads.append(pltpu.make_async_copy(h_any.at[0, 0, rows], h_buf.at[rows], in_sem.at[order]))
-        loads[-1].start()
-        if order == 0:
-            load_pattern = pltpu.make_async_copy(pattern_any, pattern_ref, in_sem.at[4])
-            load_onsite = pltpu.make_async_copy(onsite_any, onsite_ref, in_sem.at[5])
-            load_codes = pltpu.make_async_copy(code_any, code_ref, in_sem.at[6])
-            load_pattern.start()
-            load_onsite.start()
-            load_codes.start()
+    loads[1].start()
+    loads[2].start()
     load_basis = pltpu.make_async_copy(basis_any.at[0, 0], basis, in_sem.at[3])
     load_basis.start()
 
@@ -185,10 +187,8 @@
             hood[4, row, LOW[col]] = low
 
     swap = Exchange(hood, sends, recvs, 0, gx, gy, n_gx, n_gy, True)
-    load_pattern.wait()
-    load_onsite.wait()
-    load_codes.wait()
-    loads[0].wait()
+    for copy in small + [loads[0]]:
+        copy.wait()
     prepare(1)
     pl.semaphore_wait(barrier, n_gx + n_gy - 2)
     swap.begin(0, 4)
@@ -255,16 +255,18 @@
 
     def norm2(vector):
         total = sum(part * part for part in vector)
-        return jnp.sum(total, keepdims=True) + 1e-6
+        return jnp.sum(total, keepdims=True)
 
     vector = [jnp.full((B, 1), 1.0, F32) * u.astype(F32) for u in used]
+    length = jnp.ones((1, 1), F32)
     for step in range(POWER_STEPS + 1):
         image = from_rows(vector) if step % 2 == 0 else from_lanes(vector)
-        squares = norm2(image)
+        total = norm2(image)
+        factor = 1.0 / length
         if step < POWER_STEPS:
-            factor = lax.rsqrt(squares)
             vector = [part * factor for part in image]
-    estimate = jnp.sqrt(squares)
+            length = factor * jnp.sqrt(total + 1e-6 * (length * length))
+    estimate = jnp.sqrt(total * (factor * factor) + 1e-6)
     best[0] = jnp.broadcast_to(estimate, (8, B))
 
     def share(source, target, sends_to, recvs_to, count, axis):

time: 48.4 us -> 47.7 us (0.986)
  Pallas kernels: 47.4 us -> 46.8 us
    pallas_call x1, Pallas kernels: 46.7 us -> 46.1 us  [local(): pl.pallas_call(functools.partial(kernel, n_gx, n_gy), out_shape=(jax.Shap...]
where the time goes in v3:
time: 47.7 us; the launch traced here: 47.6 us
  Pallas kernels  46.8 us (98%)
  between operations  0.8 us (2%)
    pallas_call x1, Pallas kernels, local(): pl.pallas_call(functools.partial(kernel, n_gx, n_gy), out_shape=(jax.Shap...  46.1 us

profile of v3, /device:TPU:1, one launch (start us, length us, event | category | flops | bytes accessed | tf_op | source)
XLA Modules:
  0.0 47.6 jit_solution(13256369766573659695)
XLA Ops:
  0.6 46.1 %shard_map.68 = (bf16[1,1,9,128,128]{4,3,2,1,0:T(8,128)(2,1)S(1)}, f32[1,1,1024]{2,1,0:T(1,128)S(1)}) custom-call(f32[1,1,9,128,128]{4,3,2,1,0:T(8,128)} %h_any.1, f32[1,1,128]{2,1,0:T(1,128)} %onsite_any.1, s32[1,1,9]{2,1,0:T(1,128)} %pattern_any.1, s32[1,1,6]{2,1,0:T(1,128)} %code_any.1, bf16[1,1,9,1024,128]{4,3,2,1,0:T(8,128)(2,1)} %basis_any.1), custom_call_target="tpu_custom_call" | custom-call | tf_op jit(solution)/shard_map/pallas_call | solution.py:441
  46.7 0.7 %shard_map.69 = (bf16[1,1,9,128,128]{4,3,2,1,0:T(8,128)(2,1)}, f32[1,1,1024]{2,1,0:T(1,128)}) custom-call(bf16[1,1,9,128,128]{4,3,2,1,0:T(8,128)(2,1)S(1)} %get-tuple-element.4.density_in, f32[1,1,1024]{2,1,0:T(1,128)S(1)} %get-tuple-element.5.grid_in), custom_call_target="tpu_custom_call" | custom-call | tf_op jit(solution)/shard_map/pallas_call | solution.py:483

commit v4 on v3

--- a/solution.py
+++ b/solution.py
@@ -129,13 +129,9 @@
 
 def thin(matrix, high, low):
     rhs = jnp.concatenate([high, low], axis=1)
-    out = []
-    for start in range(0, ORDER, 256):
-        rows = slice(start, start + 256)
-        both = jnp.dot(matrix[0][rows, :], rhs, preferred_element_type=F32)
-        rest = jnp.dot(matrix[1][rows, :], high, preferred_element_type=F32)
-        out.append(both[:, :B] + (both[:, B:] + rest))
-    return jnp.concatenate(out, axis=0)
+    both = jnp.dot(matrix[0][...], rhs, preferred_element_type=F32)
+    rest = jnp.dot(matrix[1][...], high, preferred_element_type=F32)
+    return both[:, :B] + (both[:, B:] + rest)
 
 
 def kernel(
@@ -285,8 +281,16 @@
 
     along_x = share(0, best_x, sends_x, recvs_x, n_gx, 0)
     along_y = share(1, best_y, sends_y, recvs_y, n_gy, 1)
-    for copy in along_x:
-        copy.start()
+    def apart(step, count, width):
+        rows, row = divmod(step, width)
+        lines = count // width
+        return min(row, width - row) + min(rows, lines - rows)
+
+    def start_all(group, count, width):
+        for step in sorted(range(1, count), key=lambda n: -apart(n, count, width)):
+            group[step - 1].start()
+
+    start_all(along_x, n_gx, 2)
 
     for r in range(0, ORDER, 256):
         for c in range(r, ORDER, 256):
@@ -305,8 +309,7 @@
         copy.wait_recv()
         top = jnp.maximum(top, best_x[step])
     best[1] = top
-    for copy in along_y:
-        copy.start()
+    start_all(along_y, n_gy, 4)
 
     for r in range(0, ORDER, 256):
         for c in range(r, ORDER, 256):
@@ -354,22 +357,24 @@
             block = jnp.where(eye, 1.0, 0.0) + block
         halves[a] = 0.5 * block
     share_out = Exchange(dhood, sends, recvs, COPIES, gx, gy, n_gx, n_gy, False)
-    for code in range(9):
+    for code in (3, 4, 5, 0, 1, 2, 6, 7, 8):
         slot = jnp.int32(0)
         held = codes[0] == code
         for a in range(1, SLOTS):
             slot = jnp.where(codes[a] == code, a, slot)
             held = held | (codes[a] == code)
-        block = jnp.where(held, halves[slot], 0.0).astype(BF16)
-        dhood[4, code // 3, code % 3] = block
-        density_ref[0, 0, code] = block
-    share_out.begin(0, 12)
+        dhood[4, code // 3, code % 3] = jnp.where(held, halves[slot], 0.0).astype(BF16)
+        if code == 5:
+            share_out.begin(0, 4)
+    share_out.begin(4, 12)
     share_out.begin_x()
+    for code in range(9):
+        density_ref[0, 0, code] = dhood[4, code // 3, code % 3]
     load_basis.wait()
 
     step = 2 * lax.rem(gx, 2) - 1
 
-    def tile(near_x, near_y, first=False):
+    def tile(near_x, near_y):
         fixed = isinstance(near_x, int)
         place = (near_x + 1) * 3 + near_y + 1
         if fixed:
@@ -385,33 +390,41 @@
                     lefts.append((near_x + row) * 3 + far_y + 1)
                     rights.append(dhood[place, row, col])
         right = jnp.concatenate(rights, axis=0)
-        for start in range(0, grid_acc.shape[0], 256):
-            rows = slice(start, start + 256)
+
+        def part(rows):
             left = jnp.concatenate([basis[e, rows, :] for e in lefts], axis=1)
             product = jnp.dot(left, right, preferred_element_type=F32)
-            product = product * basis[place, rows, :].astype(F32)
-            if first:
-                grid_acc[rows, :] = product
-            else:
-                grid_acc[rows, :] = grid_acc[rows, :] + product
-
-    tile(0, 0, True)
-    share_out.forward(0, 8)
+            return product * basis[place, rows, :].astype(F32)
+
+        return part
+
+    points = grid_acc.shape[0]
+
+    def add(near_x, near_y, first=False):
+        part = tile(near_x, near_y)
+        for start in range(0, points, 256):
+            rows = slice(start, start + 256)
+            grid_acc[rows, :] = part(rows) if first else grid_acc[rows, :] + part(rows)
+
+    add(0, 0, True)
+    share_out.forward(0, 4)
     share_out.wait(share_out.along_x)
-    tile(-1, 0)
+    add(-1, 0)
+    share_out.forward(4, 8)
+    add(1, 0)
     share_out.forward(8, 12)
-    tile(1, 0)
-    tile(0, -1)
-    tile(0, 1)
+    add(0, -1)
+    add(0, 1)
     share_out.wait(share_out.to_near)
-    tile(-step, -1)
-    tile(-step, 1)
+    add(-step, -1)
+    add(-step, 1)
     share_out.wait(share_out.to_far)
-    tile(step, -1)
-    tile(step, 1)
-    for part in range(grid_acc.shape[0] // B):
-        block = grid_acc[part * B:part * B + B, :].T
-        grid_ref[0, :, pl.ds(part * B, B)] = jnp.sum(block, axis=0, keepdims=True)
+    parts = tile(step, -1), tile(step, 1)
+    for start in range(0, points, 256):
+        rows = slice(start, start + 256)
+        block = grid_acc[rows, :] + (parts[0](rows) + parts[1](rows))
+        for low in range(0, 256, B):
+            grid_ref[0, :, pl.ds(start + low, B)] = jnp.sum(block[low:low + B].T, axis=0, keepdims=True)
 
     swap.wait_sent()
     share_out.wait_sent()

time: 47.7 us -> 47.5 us (level)
  no operation moved by 1% of the time
where the time goes in v4:
time: 47.5 us; the launch traced here: 47.4 us
  Pallas kernels  46.6 us (98%)
  between operations  0.8 us (2%)
    pallas_call x1, Pallas kernels, local(): pl.pallas_call(functools.partial(kernel, n_gx, n_gy), out_shape=(jax.Shap...  45.9 us

profile of v4, /device:TPU:1, one launch (start us, length us, event | category | flops | bytes accessed | tf_op | source)
XLA Modules:
  0.0 47.4 jit_solution(8536509157254583583)
XLA Ops:
  0.6 45.9 %shard_map.68 = (bf16[1,1,9,128,128]{4,3,2,1,0:T(8,128)(2,1)S(1)}, f32[1,1,1024]{2,1,0:T(1,128)S(1)}) custom-call(f32[1,1,9,128,128]{4,3,2,1,0:T(8,128)} %h_any.1, f32[1,1,128]{2,1,0:T(1,128)} %onsite_any.1, s32[1,1,9]{2,1,0:T(1,128)} %pattern_any.1, s32[1,1,6]{2,1,0:T(1,128)} %code_any.1, bf16[1,1,9,1024,128]{4,3,2,1,0:T(8,128)(2,1)} %basis_any.1), custom_call_target="tpu_custom_call" | custom-call | tf_op jit(solution)/shard_map/pallas_call | solution.py:454
  46.5 0.7 %shard_map.69 = (bf16[1,1,9,128,128]{4,3,2,1,0:T(8,128)(2,1)}, f32[1,1,1024]{2,1,0:T(1,128)}) custom-call(bf16[1,1,9,128,128]{4,3,2,1,0:T(8,128)(2,1)S(1)} %get-tuple-element.4.density_in, f32[1,1,1024]{2,1,0:T(1,128)S(1)} %get-tuple-element.5.grid_in), custom_call_target="tpu_custom_call" | custom-call | tf_op jit(solution)/shard_map/pallas_call | solution.py:496
